TPU v7x, 32 devices: a whole 2x2x4 slice. The times are simulated.
32 devices in a mesh: groups: 2 (over x), ctx: 16 (over z, y, core).
Axes of the slice: x: 2, y: 2, z: 4, core: 2. Of those that a mesh axis runs over, the one named last changes fastest.
Arguments:
- queries: bfloat16 [4096, 2048], P(('groups', 'ctx')), parts along dimension 0, may hold values from -6 to 6
- keys: bfloat16 [4096, 2048], P(('groups', 'ctx')), parts along dimension 0, may hold values from -6 to 6
- values: bfloat16 [4096, 2048], P(('groups', 'ctx')), parts along dimension 0, may hold values from -6 to 6
- out_grad: bfloat16 [4096, 2048], P(('groups', 'ctx')), parts along dimension 0, may hold values from -6 to 6
- conv_weight: float32 [8, 16], replicated, may hold values from -2 to 2
Outputs:
- dq: bfloat16 [4096, 2048], P(('groups', 'ctx')), parts along dimension 0
- dk: bfloat16 [4096, 2048], P(('groups', 'ctx')), parts along dimension 0
- dv: bfloat16 [4096, 2048], P(('groups', 'ctx')), parts along dimension 0
- dconv: float32 [16, 16], P('groups'), parts along dimension 0
There are 2 independent parts, one for each index of `groups`. A program takes and returns all parts, laid end to end along the dimension named above; an argument that names none is the same for every part. Nothing has to cross between parts.
All inputs are finite; a program needn't handle non-finite values.
Results may differ from a plain program's by a relative error of at most 0.024.
Values may be sent and summed in bfloat16 or wider, within the bound.
A program may use at most 128 MiB of HBM per device.

v0:
```python
import jax
import jax.numpy as jnp
from jax import lax
from jax.sharding import PartitionSpec as P


def compress(rows, conv_weight):
    count = rows.shape[0]
    stride, heads = conv_weight.shape
    shaped = rows.reshape(count // stride, stride, heads, -1).astype(jnp.float32)
    merged = jnp.einsum("cshd,sh->chd", shaped, conv_weight).astype(jnp.bfloat16)
    return merged.reshape(count // stride, -1)


def local(queries, keys, values, out_grad, conv_weight):
    count, width = queries.shape
    stride, heads = conv_weight.shape
    head_dim = width // heads
    rows_mem = count // stride
    scale = head_dim ** (-0.5)
    shard_id = lax.axis_index("ctx")
    total_mem = rows_mem * lax.axis_size("ctx")
    q3 = queries.reshape(count, heads, head_dim)
    k3 = keys.reshape(count, heads, head_dim)
    v3 = values.reshape(count, heads, head_dim)
    g3 = out_grad.reshape(count, heads, head_dim)
    mem_keys = compress(keys, conv_weight)
    mem_vals = compress(values, conv_weight)
    causal = jnp.arange(count)[:, None] >= jnp.arange(count)[None, :]
    local_scores = jnp.einsum("shd,thd->hst", q3, k3, preferred_element_type=jnp.float32) * scale
    local_scores = jnp.where(causal[None], local_scores, -1e30)
    high0 = local_scores.max(-1)
    local_prob = jnp.where(causal[None], jnp.exp(local_scores - high0[..., None]), 0.0)
    total0 = local_prob.sum(-1)
    accum0 = jnp.einsum("hst,thd->hsd", local_prob, v3.astype(jnp.float32))

    def score_block(block_keys):
        rows = block_keys.shape[0]
        keys_block = block_keys.reshape(rows, heads, head_dim)
        valid = jnp.arange(rows, dtype=jnp.int32) // rows_mem < shard_id
        scores = (
            jnp.einsum("shd,nhd->hsn", q3, keys_block, preferred_element_type=jnp.float32) * scale
        )
        return (valid, scores)

    all_keys, all_vals = (
        lax.all_gather(mem_keys, "ctx", axis=0, tiled=True),
        lax.all_gather(mem_vals, "ctx", axis=0, tiled=True),
    )
    high = high0
    total = total0
    accum = accum0
    rows = all_keys.shape[0]
    valid, scores = score_block(all_keys)
    scores = jnp.where(valid[None, None, :], scores, -1e30)
    new_high = jnp.maximum(high, scores.max(-1))
    prob = jnp.where(valid[None, None, :], jnp.exp(scores - new_high[..., None]), 0.0)
    factor = jnp.exp(high - new_high)
    vals_block = all_vals.reshape(rows, heads, head_dim)
    total = total * factor + prob.sum(-1)
    accum = accum * factor[..., None] + jnp.einsum(
        "hsn,nhd->hsd", prob, vals_block, preferred_element_type=jnp.float32
    )
    stats = (new_high, total, accum)
    high, total, accum = stats
    lse = high + jnp.log(total)
    output = accum / total[..., None]
    dsum = jnp.einsum("hsd,shd->hs", output, g3.astype(jnp.float32))
    valid_all, scores_all = score_block(all_keys)
    mem_prob = jnp.where(valid_all[None, None, :], jnp.exp(scores_all - lse[..., None]), 0.0)
    keys_all = all_keys.reshape(total_mem, heads, head_dim)
    vals_all = all_vals.reshape(total_mem, heads, head_dim)
    mem_dprob = jnp.einsum("shd,nhd->hsn", g3, vals_all, preferred_element_type=jnp.float32)
    mem_ds = (mem_prob * (mem_dprob - dsum[..., None])).astype(jnp.bfloat16)
    mem_pb = mem_prob.astype(jnp.bfloat16)
    dq_mem = jnp.einsum("hsn,nhd->shd", mem_ds, keys_all, preferred_element_type=jnp.float32)
    dk_part = jnp.einsum("hsn,shd->nhd", mem_ds, q3, preferred_element_type=jnp.float32) * scale
    dv_part = jnp.einsum("hsn,shd->nhd", mem_pb, g3, preferred_element_type=jnp.float32)
    summed = lax.psum_scatter(
        jnp.concatenate(
            (dk_part.reshape(total_mem, width), dv_part.reshape(total_mem, width)), axis=1
        ),
        "ctx",
        scatter_dimension=0,
        tiled=True,
    )
    dmem_k = summed[:, :width].reshape(rows_mem, heads, head_dim)
    dmem_v = summed[:, width:].reshape(rows_mem, heads, head_dim)
    local_p = jnp.where(causal[None], jnp.exp(local_scores - lse[..., None]), 0.0)
    local_dp = jnp.einsum("shd,thd->hst", g3, v3, preferred_element_type=jnp.float32)
    local_ds = (local_p * (local_dp - dsum[..., None])).astype(jnp.bfloat16)
    dq_all = (
        dq_mem + jnp.einsum("hst,thd->shd", local_ds, k3, preferred_element_type=jnp.float32)
    ) * scale
    dk_local = jnp.einsum("hst,shd->thd", local_ds, q3, preferred_element_type=jnp.float32) * scale
    dv_local = jnp.einsum(
        "hst,shd->thd", local_p.astype(jnp.bfloat16), g3, preferred_element_type=jnp.float32
    )
    spread_k = jnp.einsum("chd,sh->cshd", dmem_k, conv_weight).reshape(count, heads, head_dim)
    spread_v = jnp.einsum("chd,sh->cshd", dmem_v, conv_weight).reshape(count, heads, head_dim)
    dq = dq_all.reshape(count, width).astype(jnp.bfloat16)
    dk = (dk_local + spread_k).reshape(count, width).astype(jnp.bfloat16)
    dv = (dv_local + spread_v).reshape(count, width).astype(jnp.bfloat16)
    key_rows = keys.reshape(rows_mem, stride, heads, head_dim).astype(jnp.float32)
    val_rows = values.reshape(rows_mem, stride, heads, head_dim).astype(jnp.float32)
    partial_conv = jnp.einsum("chd,cshd->sh", dmem_k, key_rows) + jnp.einsum(
        "chd,cshd->sh", dmem_v, val_rows
    )
    dconv = lax.psum(partial_conv, "ctx")
    return (dq, dk, dv, dconv)


def solution(mesh):
    return jax.shard_map(
        local,
        mesh=mesh,
        in_specs=(
            P(("groups", "ctx"), None),
            P(("groups", "ctx"), None),
            P(("groups", "ctx"), None),
            P(("groups", "ctx"), None),
            P(),
        ),
        out_specs=(
            P(("groups", "ctx"), None),
            P(("groups", "ctx"), None),
            P(("groups", "ctx"), None),
            P("groups", None),
        ),
        check_vma=False,
    )
```

profile of v0, /device:TPU:0, one launch (start us, length us, event | category | flops | bytes accessed | tf_op | source)
XLA Modules:
  0.0 238.7 jit_solution(13422166051931242764)
XLA Ops:
  7.2 0.0 copy-start.4
  7.2 0.0 all-gather.3.cloned.1.call-start
  7.2 0.8 copy.90
  8.1 1.4 fusion.38
  9.5 0.6 copy.159
  10.2 0.0 all-gather.3.cloned.1.call-update
  10.2 0.0 all-gather.5.cloned.1.call-start
  10.2 1.3 fusion.36
  11.6 0.6 copy.158
  12.3 0.0 all-gather.5.cloned.1.call-update
  12.3 0.0 reduce-scatter.4.cloned.1.call-start
  12.3 0.3 copy.134
  12.6 0.3 copy.133
  12.9 0.1 copy.138
  13.0 1.2 copy.80
  14.3 0.4 fusion.57
  14.7 1.0 copy-done
  15.7 0.2 fusion.31
  15.9 35.5 %all-gather.3.cloned.1.call-done = bf16[256,2048]{1,0:T(8,128)(2,1)} async-done(((bf16[16,2048]{1,0:T(8,128)(2,1)}), bf16[256,2048]{1,0:T(8,128)(2,1)}) %all-gather.3.cloned.1.call-update) | async-done | bytes 1048592 | tf_op jit(solution)/shard_map/all_gather | solution.py:47
  51.4 2.3 copy.58
  53.6 1.8 bitcast_reduce_fusion
  55.5 0.6 fusion.5
  56.1 34.3 %all-gather.5.cloned.1.call-done = bf16[256,2048]{1,0:T(8,128)(2,1)} async-done(((bf16[16,2048]{1,0:T(8,128)(2,1)}), bf16[256,2048]{1,0:T(8,128)(2,1)}) %all-gather.5.cloned.1.call-update) | async-done | bytes 1048592 | tf_op jit(solution)/shard_map/all_gather | solution.py:48
  90.4 2.3 copy.63
  92.7 2.2 fusion.3
  94.9 0.8 fusion.13
  95.8 0.7 multiply_reduce_fusion.2
  96.5 0.1 copy.105
  96.5 3.1 %fusion.19 = f32[16,256,128]{1,2,0:T(8,128)} fusion(bf16[128,16,128]{0,2,1:T(8,128)(2,1)} %copy.80, f32[16,256,128]{2,1,0:T(8,128)S(1)} %get-tuple-element.26, f32[16,128]{1,0:T(8,128)S(1)} %get-tuple-element.16, pred[256]{0:T(512)(128)(4,1)S(1)} %fusion.48), kind=kOutput, calls=%fused_computation.31 | convolution fusion | flops 136314880 | bytes 4727040 | tf_op jit(solution)/shard_map/hsn,shd->nhd/dot_general | solution.py:78
  99.6 0.9 multiply_convert_fusion
  100.5 1.0 copy-done.10
  101.5 0.4 multiply_bitcast_fusion
  101.9 1.8 copy.79
  103.7 4.5 %pad_maximum_fusion = f32[256,4096]{0,1:T(8,128)} fusion(f32[256,2048]{0,1:T(8,128)} %bitcast.140, f32[256,2048]{0,1:T(8,128)} %bitcast.141), kind=kLoop, calls=%fused_computation | loop fusion | flops 1048576 | bytes 8388608 | tf_op jit(solution)/shard_map/concatenate | solution.py:80
  108.2 5.6 %copy.125 = f32[256,4096]{1,0:T(8,128)} copy(f32[256,4096]{0,1:T(8,128)} %pad_maximum_fusion) | data formatting | bytes 8388608
  113.8 0.0 reduce-scatter.4.cloned.1.call-update
  113.8 1.2 copy-done.2
  115.0 1.6 fusion.17
  116.6 0.1 copy-done.11
  116.7 0.4 convolution_bitcast_fusion.2
  117.2 0.8 copy-done.9
  118.0 0.3 fusion.16
  118.3 1.0 copy.87
  119.3 66.5 %reduce-scatter.4.cloned.1.call-done = f32[16,4096]{1,0:T(8,128)} async-done(((f32[256,4096]{1,0:T(8,128)}), f32[16,4096]{1,0:T(8,128)}) %reduce-scatter.4.cloned.1.call-update) | async-done | bytes 262160
  185.8 1.0 fusion.56
  186.8 0.3 copy.128
  187.1 0.3 copy.85
  187.4 0.3 copy.130
  187.8 1.3 multiply_reduce_fusion
  189.0 0.7 copy.124
  189.7 0.3 copy.127
  190.0 0.3 copy.81
  190.4 0.3 copy.129
  190.7 0.2 multiply_reduce_fusion.1
  190.9 0.1 copy.117
  191.0 0.7 add_bitcast_fusion
  191.6 30.1 %psum.7 = f32[8,16]{1,0:T(8,128)} all-reduce(f32[8,16]{1,0:T(8,128)S(1)} %add_bitcast_fusion), channel_id=1, replica_groups=mesh['groups'=2,'ctx'=16] {'ctx'}, use_global_device_ids=true, to_apply=%region_5.6 | all-reduce | flops 128 | bytes 1024 | tf_op jit(solution)/shard_map/psum | solution.py:109
  221.7 2.4 broadcast_multiply_fusion
  224.1 1.6 copy.86
  225.7 1.3 fusion.18
  227.0 2.1 copy.89
  229.1 1.6 copy.82
  230.7 0.5 fusion.15
  231.2 1.0 copy.88
  (40 shorter events, 0.2 us)
Async XLA Ops:
  7.2 5.2 %copy-start.4 = (bf16[128,2048]{1,0:T(8,128)(2,1)S(1)}, bf16[128,2048]{1,0:T(8,128)(2,1)}, u32[]{:S(2)}) copy-start(bf16[128,2048]{1,0:T(8,128)(2,1)} %param.6) | copy-start | bytes 1572868
  7.2 5.5 %copy-start.16 = (bf16[128,2048]{1,0:T(8,128)(2,1)S(1)}, bf16[128,2048]{1,0:T(8,128)(2,1)}, u32[]{:S(2)}) copy-start(bf16[128,2048]{1,0:T(8,128)(2,1)} %param.5) | copy-start | bytes 1572868
  7.2 44.2 %all-gather.3.cloned.1.call-start = ((), (), s32[]{:S(2)}) async-start(), calls=%async_computation.1 | async-start | bytes 1114112 | tf_op jit(solution)/shard_map/all_gather | solution.py:47
  8.1 4.8 %copy-start.17 = (bf16[128,2048]{1,0:T(8,128)(2,1)S(1)}, bf16[128,2048]{1,0:T(8,128)(2,1)}, u32[]{:S(2)}) copy-start(bf16[128,2048]{1,0:T(8,128)(2,1)} %param.8) | copy-start | bytes 1572868
  10.2 80.2 %all-gather.5.cloned.1.call-start = ((), (), s32[]{:S(2)}) async-start(), calls=%async_computation.2 | async-start | bytes 1114112 | tf_op jit(solution)/shard_map/all_gather | solution.py:48
  12.3 173.5 %reduce-scatter.4.cloned.1.call-start = ((), (), s32[]{:S(2)}) async-start(), calls=%async_computation.3 | async-start | bytes 4456448
  12.6 2.1 copy-start.8
  14.7 1.0 copy-start
  92.7 2.2 copy-start.1
  92.7 2.2 copy-start.14
  94.9 19.0 %copy-start.18 = (f32[16,128]{1,0:T(8,128)}, f32[16,128]{1,0:T(8,128)S(1)}, u32[]{:S(2)}) copy-start(f32[16,128]{1,0:T(8,128)S(1)} %get-tuple-element.16) | copy-start | bytes 24580
  96.5 3.1 %copy-start.6 = (bf16[128,16,128]{0,2,1:T(8,128)(2,1)S(1)}, bf16[128,16,128]{0,2,1:T(8,128)(2,1)}, u32[]{:S(2)}) copy-start(bf16[128,16,128]{0,2,1:T(8,128)(2,1)} %copy.80) | copy-start | bytes 1572868
  96.5 3.1 %copy-start.15 = (bf16[256,2048]{0,1:T(8,128)(2,1)S(1)}, bf16[256,2048]{0,1:T(8,128)(2,1)}, u32[]{:S(2)}) copy-start(bf16[256,2048]{0,1:T(8,128)(2,1)} %copy.63) | copy-start | bytes 3145732
  100.5 1.0 copy-start.10
  113.8 1.2 copy-start.2
  115.0 1.6 copy-start.3
  115.0 1.7 copy-start.11
  116.7 1.5 copy-start.12
  116.7 1.2 copy-start.9
  187.7 2.9 %copy-start.5 = (bf16[128,2048]{1,0:T(8,128)(2,1)S(1)}, bf16[128,2048]{1,0:T(8,128)(2,1)}, u32[]{:S(2)}) copy-start(bf16[128,2048]{1,0:T(8,128)(2,1)} %param.6) | copy-start | bytes 1572868
  221.7 4.0 %copy-start.7 = (bf16[128,16,128]{0,2,1:T(8,128)(2,1)S(1)}, bf16[128,16,128]{0,2,1:T(8,128)(2,1)}, u32[]{:S(2)}) copy-start(bf16[128,16,128]{0,2,1:T(8,128)(2,1)} %copy.80) | copy-start | bytes 1572868
  221.7 4.0 %copy-start.19 = (f32[16,128]{1,0:T(8,128)S(1)}, f32[16,128]{1,0:T(8,128)}, u32[]{:S(2)}) copy-start(f32[16,128]{1,0:T(8,128)} %copy-done.18) | copy-start | bytes 24580
  227.0 3.7 %copy-start.13 = (bf16[16,128,128]{1,2,0:T(8,128)(2,1)S(1)}, bf16[16,128,128]{1,2,0:T(8,128)(2,1)}, u32[]{:S(2)}) copy-start(bf16[16,128,128]{1,2,0:T(8,128)(2,1)} %copy-done.12) | copy-start | bytes 1572868
Sparse Core Ops, SparseCore 0:
  10.7 40.5 all-gather.2
  53.5 36.8 all-gather.4
  114.0 71.7 reduce-scatter.3
where the time goes:
time: 239 us
  waiting for transfers between devices  136 us (57%)
  local copies, waits for them, and re-layouts  31.1 us (13%)
  blocking collectives  30.1 us (13%)
  matrix products  16.4 us (7%)
  between operations  14.1 us (6%)
  other arithmetic  10.6 us (4%)
    unnamed x4, waiting for transfers between devices  66.5 us
    all_gather x1, waiting for transfers between devices, local(): lax.all_gather(mem_keys, 'ctx', axis=0, tiled=True)  35.5 us
    all_gather x1, waiting for transfers between devices, local(): lax.all_gather(mem_vals, 'ctx', axis=0, tiled=True)  34.3 us
    psum x1, blocking collectives, local(): dconv = lax.psum(partial_conv, 'ctx')  30.1 us
    unnamed x52, local copies, waits for them, and re-layouts  17.3 us
  transfers between devices with their start and end apart: 3, of which 3 were waited for; matrix products, arithmetic and copies ran while one was open for 5% of the time, Pallas kernels for 0%

commit v1 on v0

--- a/solution.py
+++ b/solution.py
@@ -106,7 +106,9 @@
     partial_conv = jnp.einsum("chd,cshd->sh", dmem_k, key_rows) + jnp.einsum(
         "chd,cshd->sh", dmem_v, val_rows
     )
-    dconv = lax.psum(partial_conv, "ctx")
+    dconv = partial_conv
+    for hop in (1, 2, 4, 8):
+        dconv = dconv + lax.ppermute(dconv, "ctx", [(dev, dev ^ hop) for dev in range(16)])
     return (dq, dk, dv, dconv)
 
 

time: 239 us -> 218 us (0.912)
  blocking collectives: 30.1 us -> 0 us
  matrix products: 16.4 us -> 20.7 us
  starting transfers between devices: 0.12 us -> 3.85 us
    psum x1 -> x0, blocking collectives: 30.1 us -> none  [local(): dconv = lax.psum(partial_conv, 'ctx')]
    ppermute x0 -> x4, starting transfers between devices: none -> 3.73 us  [local(): lax.ppermute(dconv, 'ctx', [(dev, dev ^ hop) for dev in range(16)])]
    unnamed x52 -> x46, local copies, waits for them, and re-layouts: 17.3 us -> 17.6 us
  transfers between devices with their start and end apart: 3 -> 7, of which waited for: 3 -> 3; matrix products, arithmetic and copies ran while one was open for 5% -> 13% of each run, Pallas kernels for 0% -> 0%
where the time goes in v1:
time: 218 us; the launch traced here: 217 us
  waiting for transfers between devices  137 us (63%)
  local copies, waits for them, and re-layouts  32.1 us (15%)
  matrix products  20.7 us (9%)
  between operations  14.1 us (6%)
  other arithmetic  9.73 us (4%)
  starting transfers between devices  3.85 us (2%)
    unnamed x4, waiting for transfers between devices  67 us
    all_gather x1, waiting for transfers between devices, local(): lax.all_gather(mem_keys, 'ctx', axis=0, tiled=True)  35.5 us
    all_gather x1, waiting for transfers between devices, local(): lax.all_gather(mem_vals, 'ctx', axis=0, tiled=True)  34.2 us
    unnamed x46, local copies, waits for them, and re-layouts  17.6 us
    concatenate x1, other arithmetic, local(): jnp.concatenate((dk_part.reshape(total_mem, width), dv_part.reshape(total...  4.46 us
  transfers between devices with their start and end apart: 7, of which 3 were waited for; matrix products, arithmetic and copies ran while one was open for 13% of the time, Pallas kernels for 0%

profile of v1, /device:TPU:0, one launch (start us, length us, event | category | flops | bytes accessed | tf_op | source)
XLA Modules:
  0.0 217.2 jit_solution(4071601867993659151)
XLA Ops:
  7.2 0.0 copy-start.4
  7.2 0.0 all-gather.3.cloned.1.call-start
  7.2 0.8 copy.90
  8.1 1.4 fusion.38
  9.5 0.6 copy.159
  10.2 0.0 all-gather.3.cloned.1.call-update
  10.2 0.0 all-gather.5.cloned.1.call-start
  10.2 1.3 fusion.36
  11.6 0.6 copy.158
  12.3 0.0 all-gather.5.cloned.1.call-update
  12.3 0.0 reduce-scatter.4.cloned.1.call-start
  12.3 0.3 copy.134
  12.6 0.3 copy.133
  12.9 0.1 copy.138
  13.1 1.2 copy.80
  14.3 0.4 fusion.57
  14.7 0.9 copy-done
  15.6 0.2 fusion.31
  15.8 35.5 %all-gather.3.cloned.1.call-done = bf16[256,2048]{1,0:T(8,128)(2,1)} async-done(((bf16[16,2048]{1,0:T(8,128)(2,1)}), bf16[256,2048]{1,0:T(8,128)(2,1)}) %all-gather.3.cloned.1.call-update) | async-done | bytes 1048592 | tf_op jit(solution)/shard_map/all_gather | solution.py:47
  51.4 2.3 %copy.58 = bf16[256,2048]{0,1:T(8,128)(2,1)} copy(bf16[256,2048]{1,0:T(8,128)(2,1)} %all-gather.3.cloned.1.call-done) | data formatting | bytes 2097152 | tf_op jit(solution)/shard_map/all_gather | solution.py:47
  53.7 1.8 bitcast_reduce_fusion
  55.5 0.6 fusion.5
  56.1 34.2 %all-gather.5.cloned.1.call-done = bf16[256,2048]{1,0:T(8,128)(2,1)} async-done(((bf16[16,2048]{1,0:T(8,128)(2,1)}), bf16[256,2048]{1,0:T(8,128)(2,1)}) %all-gather.5.cloned.1.call-update) | async-done | bytes 1048592 | tf_op jit(solution)/shard_map/all_gather | solution.py:48
  90.4 2.3 %copy.63 = bf16[256,2048]{0,1:T(8,128)(2,1)} copy(bf16[256,2048]{1,0:T(8,128)(2,1)} %all-gather.5.cloned.1.call-done) | data formatting | bytes 2097152 | tf_op jit(solution)/shard_map/all_gather | solution.py:48
  92.7 2.2 %fusion.3 = f32[16,128,128]{2,1,0:T(8,128)S(1)} fusion(bf16[256,16,128]{0,2,1:T(8,128)(2,1)} %bitcast.151, f32[16,256,128]{2,1,0:T(8,128)S(1)} %get-tuple-element.26, f32[16,128]{1,0:T(8,128)S(1)} %max.16, pred[256]{0:T(512)(128)(4,1)S(1)} %fusion.48), kind=kOutput, calls=%fused_computation.9 | convolution fusion | flops 136314880 | bytes 4202752 | tf_op jit(solution)/shard_map/hsn,nhd->hsd/dot_general | solution.py:61
  94.9 0.8 fusion.13
  95.7 0.7 multiply_reduce_fusion.2
  96.5 0.1 copy.105
  96.5 3.1 %fusion.19 = f32[16,256,128]{1,2,0:T(8,128)} fusion(bf16[128,16,128]{0,2,1:T(8,128)(2,1)} %copy.80, f32[16,256,128]{2,1,0:T(8,128)S(1)} %get-tuple-element.26, f32[16,128]{1,0:T(8,128)S(1)} %get-tuple-element.16, pred[256]{0:T(512)(128)(4,1)S(1)} %fusion.48), kind=kOutput, calls=%fused_computation.31 | convolution fusion | flops 136314880 | bytes 4727040 | tf_op jit(solution)/shard_map/hsn,shd->nhd/dot_general | solution.py:78
  99.6 0.8 multiply_convert_fusion
  100.4 1.0 copy-done.9
  101.4 0.4 multiply_bitcast_fusion
  101.9 1.8 copy.79
  103.7 4.5 %pad_maximum_fusion = f32[256,4096]{0,1:T(8,128)} fusion(f32[256,2048]{0,1:T(8,128)} %bitcast.140, f32[256,2048]{0,1:T(8,128)} %bitcast.141), kind=kLoop, calls=%fused_computation | loop fusion | flops 1048576 | bytes 8388608 | tf_op jit(solution)/shard_map/concatenate | solution.py:80
  108.2 5.6 %copy.125 = f32[256,4096]{1,0:T(8,128)} copy(f32[256,4096]{0,1:T(8,128)} %pad_maximum_fusion) | data formatting | bytes 8388608
  113.8 0.0 reduce-scatter.4.cloned.1.call-update
  113.8 1.2 copy-done.2
  115.0 2.4 %fusion.17 = bf16[16,128,128]{1,2,0:T(8,128)(2,1)} fusion(bf16[128,16,128]{0,2,1:T(8,128)(2,1)S(1)} %copy-done.6, f32[16,128,128]{1,2,0:T(8,128)S(1)} %copy-done.2, f32[16,128]{1,0:T(8,128)S(1)} %copy.105, f32[16,128]{1,0:T(8,128)S(1)} %get-tuple-element.16, pred[128,128]{0,1:T(8,128)(4,1)S(1)} %iota_compare_fusion, bf16[128,2048]{1,0:T(8,128)(2,1)} %param.7), kind=kOutput, calls=%fused_computation.29 | convolution fusion | flops 68419584 | bytes 2654208 | tf_op jit(solution)/shard_map/shd,thd->hst/dot_general | solution.py:90
  117.4 1.4 convolution_bitcast_fusion.2
  118.8 66.9 %reduce-scatter.4.cloned.1.call-done = f32[16,4096]{1,0:T(8,128)} async-done(((f32[256,4096]{1,0:T(8,128)}), f32[16,4096]{1,0:T(8,128)}) %reduce-scatter.4.cloned.1.call-update) | async-done | bytes 262160
  185.7 1.0 fusion.56
  186.7 0.3 copy.128
  187.1 0.3 copy.130
  187.4 1.2 multiply_reduce_fusion
  188.6 0.1 copy.124
  188.7 1.3 copy.127
  190.0 1.5 copy.129
  191.6 0.2 multiply_reduce_fusion.1
  191.8 0.1 copy.117
  191.8 1.8 fusion.16
  193.7 1.0 copy.87
  194.7 0.3 copy.85
  195.0 1.5 copy.81
  196.6 0.5 collective-permute-start.1
  197.1 1.6 broadcast_multiply_fusion
  198.8 1.6 copy.86
  200.4 2.1 collective-permute-start.2
  202.5 1.3 fusion.18
  203.8 1.6 copy.82
  205.4 1.1 collective-permute-start.3
  206.5 1.5 fusion.15
  208.1 1.0 copy.89
  209.1 1.0 copy.88
  210.1 0.6 add.65
  (45 shorter events, 0.2 us)
Async XLA Ops:
  7.2 5.2 %copy-start.4 = (bf16[128,2048]{1,0:T(8,128)(2,1)S(1)}, bf16[128,2048]{1,0:T(8,128)(2,1)}, u32[]{:S(2)}) copy-start(bf16[128,2048]{1,0:T(8,128)(2,1)} %param.6) | copy-start | bytes 1572868
  7.2 5.5 %copy-start.14 = (bf16[128,2048]{1,0:T(8,128)(2,1)S(1)}, bf16[128,2048]{1,0:T(8,128)(2,1)}, u32[]{:S(2)}) copy-start(bf16[128,2048]{1,0:T(8,128)(2,1)} %param.5) | copy-start | bytes 1572868
  7.2 44.2 %all-gather.3.cloned.1.call-start = ((), (), s32[]{:S(2)}) async-start(), calls=%async_computation.1 | async-start | bytes 1114112 | tf_op jit(solution)/shard_map/all_gather | solution.py:47
  8.1 4.8 %copy-start.15 = (bf16[128,2048]{1,0:T(8,128)(2,1)S(1)}, bf16[128,2048]{1,0:T(8,128)(2,1)}, u32[]{:S(2)}) copy-start(bf16[128,2048]{1,0:T(8,128)(2,1)} %param.8) | copy-start | bytes 1572868
  10.2 80.2 %all-gather.5.cloned.1.call-start = ((), (), s32[]{:S(2)}) async-start(), calls=%async_computation.2 | async-start | bytes 1114112 | tf_op jit(solution)/shard_map/all_gather | solution.py:48
  12.3 173.5 %reduce-scatter.4.cloned.1.call-start = ((), (), s32[]{:S(2)}) async-start(), calls=%async_computation.3 | async-start | bytes 4456448
  12.6 2.1 copy-start.8
  14.7 1.0 copy-start
  92.7 2.2 %copy-start.1 = (f32[16,128,128]{1,2,0:T(8,128)S(1)}, f32[16,128,128]{1,2,0:T(8,128)}, u32[]{:S(2)}) copy-start(f32[16,128,128]{1,2,0:T(8,128)} %copy-done) | copy-start | bytes 3145732
  92.7 2.2 %copy-start.11 = (bf16[128,2048]{1,0:T(8,128)(2,1)S(1)}, bf16[128,2048]{1,0:T(8,128)(2,1)}, u32[]{:S(2)}) copy-start(bf16[128,2048]{1,0:T(8,128)(2,1)} %param.7) | copy-start | bytes 1572868
  96.5 3.1 %copy-start.6 = (bf16[128,16,128]{0,2,1:T(8,128)(2,1)S(1)}, bf16[128,16,128]{0,2,1:T(8,128)(2,1)}, u32[]{:S(2)}) copy-start(bf16[128,16,128]{0,2,1:T(8,128)(2,1)} %copy.80) | copy-start | bytes 1572868
  96.5 3.1 %copy-start.13 = (bf16[256,2048]{0,1:T(8,128)(2,1)S(1)}, bf16[256,2048]{0,1:T(8,128)(2,1)}, u32[]{:S(2)}) copy-start(bf16[256,2048]{0,1:T(8,128)(2,1)} %copy.63) | copy-start | bytes 3145732
  100.4 1.0 copy-start.9
  113.8 1.2 copy-start.2
  115.0 2.4 %copy-start.3 = (bf16[256,2048]{0,1:T(8,128)(2,1)S(1)}, bf16[256,2048]{0,1:T(8,128)(2,1)}, u32[]{:S(2)}) copy-start(bf16[256,2048]{0,1:T(8,128)(2,1)} %copy.58) | copy-start | bytes 3145732
  115.0 2.4 %copy-start.10 = (bf16[16,256,128]{2,1,0:T(8,128)(2,1)S(1)}, bf16[16,256,128]{2,1,0:T(8,128)(2,1)}, u32[]{:S(2)}) copy-start(bf16[16,256,128]{2,1,0:T(8,128)(2,1)} %copy-done.9) | copy-start | bytes 3145732
  187.1 4.5 %copy-start.5 = (bf16[128,2048]{1,0:T(8,128)(2,1)S(1)}, bf16[128,2048]{1,0:T(8,128)(2,1)}, u32[]{:S(2)}) copy-start(bf16[128,2048]{1,0:T(8,128)(2,1)} %param.6) | copy-start | bytes 1572868
  191.8 4.7 %collective-permute-start = (f32[8,16]{1,0:T(8,128)S(1)}, f32[8,16]{1,0:T(8,128)S(1)}, u32[]{:S(2)}, u32[]{:S(2)}) collective-permute-start(f32[8,16]{1,0:T(8,128)S(1)} %add_bitcast_fusion), channel_id=1, source_target_pairs={{0,1},{1,0},{2,3},{3,2},{4,5},{5,4},{6,7},{7,6},{8,9},{9,8},{10,11... | collective-permute-start | bytes 1544 | tf_op jit(solution)/shard_map/ppermute | solution.py:111
  193.7 3.4 %copy-start.16 = (f32[8,16]{1,0:T(8,128)S(1)}, f32[8,16]{1,0:T(8,128)}, u32[]{:S(2)}) copy-start(f32[8,16]{1,0:T(8,128)} %param.9) | copy-start | bytes 1540
  196.6 3.8 %collective-permute-start.1 = (f32[8,16]{1,0:T(8,128)S(1)}, f32[8,16]{1,0:T(8,128)S(1)}, u32[]{:S(2)}, u32[]{:S(2)}) collective-permute-start(f32[8,16]{1,0:T(8,128)S(1)} %add.62), channel_id=1, source_target_pairs={{0,2},{1,3},{2,0},{3,1},{4,6},{5,7},{6,4},{7,5},{8,10},{9,11},{10,... | collective-permute-start | bytes 1544 | tf_op jit(solution)/shard_map/ppermute | solution.py:111
  197.1 5.3 %copy-start.7 = (bf16[128,16,128]{0,2,1:T(8,128)(2,1)S(1)}, bf16[128,16,128]{0,2,1:T(8,128)(2,1)}, u32[]{:S(2)}) copy-start(bf16[128,16,128]{0,2,1:T(8,128)(2,1)} %copy.80) | copy-start | bytes 1572868
  200.4 5.0 %collective-permute-start.2 = (f32[8,16]{1,0:T(8,128)S(1)}, f32[8,16]{1,0:T(8,128)S(1)}, u32[]{:S(2)}, u32[]{:S(2)}) collective-permute-start(f32[8,16]{1,0:T(8,128)S(1)} %add.63), channel_id=1, source_target_pairs={{0,4},{1,5},{2,6},{3,7},{4,0},{5,1},{6,2},{7,3},{8,12},{9,13},{10,... | collective-permute-start | bytes 1544 | tf_op jit(solution)/shard_map/ppermute | solution.py:111
  203.7 4.3 %copy-start.12 = (bf16[128,16,128]{0,2,1:T(8,128)(2,1)S(1)}, bf16[128,16,128]{0,2,1:T(8,128)(2,1)}, u32[]{:S(2)}) copy-start(bf16[128,16,128]{0,2,1:T(8,128)(2,1)} %fusion.18) | copy-start | bytes 1572868
  205.4 4.7 %collective-permute-start.3 = (f32[8,16]{1,0:T(8,128)S(1)}, f32[8,16]{1,0:T(8,128)S(1)}, u32[]{:S(2)}, u32[]{:S(2)}) collective-permute-start(f32[8,16]{1,0:T(8,128)S(1)} %add.64), channel_id=1, source_target_pairs={{0,8},{1,9},{2,10},{3,11},{4,12},{5,13},{6,14},{7,15},{8,0},{9,1},... | collective-permute-start | bytes 1544 | tf_op jit(solution)/shard_map/ppermute | solution.py:111
Sparse Core Ops, SparseCore 0:
  10.7 40.5 all-gather.2
  53.5 36.8 all-gather.4
  114.0 71.7 reduce-scatter.3
